TPU v7x, 128 devices: a whole 4x4x4 slice. The times are simulated.
128 devices in a mesh: gz: 8 (over x, z_hi), tile: 16 (over z_lo, y, core).
Axes of the slice: x: 4, y: 4, z: 4 (z_hi: 2, z_lo: 2; z = z_hi * 2 + z_lo), core: 2. Of those that a mesh axis runs over, the one named last changes fastest.
Arguments:
- disp: float32 [16, 2, 128, 5120], P('gz', None, 'tile'), may hold values from -6 to 6
- vel: float32 [16, 2, 128, 5120], P('gz', None, 'tile'), may hold values from -4 to 4
- stiff_class: int32 [16, 128, 5120], P('gz', 'tile'), may hold values from 0 to 7
- valid: int32 [16, 128, 5120], P('gz', 'tile'), may hold values 0 or 1
- class_table: float32 [8], replicated, may hold values from 0.3 to 3
- warp: float32 [16, 3, 2], P('gz'), may hold values from 0 to 1
- spring_z: float32 [16, 3], P('gz'), may hold values from 1.2 to 2
- skip_partner: int32 [16], replicated, may hold values from 0 to 15, as said below
Outputs:
- disp_out: float32 [16, 2, 128, 5120], P('gz', None, 'tile')
- vel_out: float32 [16, 2, 128, 5120], P('gz', None, 'tile')
Inputs may be any that keep to these rules, and one draw needn't show every extreme that they name: `skip_partner`: each section's partner lies in another z-block of 2 consecutive sections; the sections of one z-block have at most 1 partners inside any one other z-block, and exactly 1 inside some.
All inputs are finite; a program needn't handle non-finite values. No bound on the sum of `valid` on one device may be relied on, other than what follows from the above.
Results may differ from a plain program's by a relative error of at most 0.0003.
Values sent between devices are 32-bit elements; how exact they have to be, the bound alone decides.
A program may use at most 128 MiB of HBM per device.

v0:
```python
import jax
import jax.numpy as jnp
from jax import lax
from jax.sharding import PartitionSpec as P

ITERS = 3
DAMPING = 0.9
STEP = 0.1


def extended(block, sides, width):
    for axis, dim in sides:
        count = lax.axis_size(axis)
        forward = [(i, i + 1) for i in range(count - 1)]
        backward = [(target, source) for source, target in forward]
        low = lax.ppermute(
            lax.slice_in_dim(block, block.shape[dim] - width, None, axis=dim), axis, forward
        )
        high = lax.ppermute(lax.slice_in_dim(block, 0, width, axis=dim), axis, backward)
        block = jnp.concatenate([low, block, high], axis=dim)
    return block


def shift_left(field):
    return jnp.concatenate([field[..., 1:], jnp.zeros_like(field[..., :1])], axis=-1)


def shift_right(field):
    return jnp.concatenate([jnp.zeros_like(field[..., :1]), field[..., :-1]], axis=-1)


def warped(source, frac_row, frac_col):
    frac_row = frac_row[:, None, None, None]
    frac_col = frac_col[:, None, None, None]
    upper = source[:, :, 1:-1]
    lower = source[:, :, 2:]
    return (
        (1.0 - frac_row) * (1.0 - frac_col) * upper
        + (1.0 - frac_row) * frac_col * shift_left(upper)
        + frac_row * (1.0 - frac_col) * lower
        + frac_row * frac_col * shift_left(lower)
    )


def section_force(
    field_ext, stiff_ext, prev_ext, next_ext, partner_ext, warp, spring_z, has_prev, has_next
):
    center = field_ext[:, :, 1:-1]
    stiff_mid = stiff_ext[:, None, 1:-1]
    stiff_up = stiff_ext[:, None, :-2]
    stiff_down = stiff_ext[:, None, 2:]
    inplane = stiff_mid * (
        stiff_up * (field_ext[:, :, :-2] - center)
        + stiff_down * (field_ext[:, :, 2:] - center)
        + shift_right(stiff_mid) * (shift_right(center) - center)
        + shift_left(stiff_mid) * (shift_left(center) - center)
    )
    pull = (
        spring_z[:, 0][:, None, None, None]
        * has_prev[:, None, None, None]
        * (warped(prev_ext, warp[:, 0, 0], warp[:, 0, 1]) - center)
    )
    pull = pull + spring_z[:, 1][:, None, None, None] * has_next[:, None, None, None] * (
        warped(next_ext, warp[:, 1, 0], warp[:, 1, 1]) - center
    )
    pull = pull + spring_z[:, 2][:, None, None, None] * (
        warped(partner_ext, warp[:, 2, 0], warp[:, 2, 1]) - center
    )
    return inplane + pull


def body(disp, vel, stiff_class, valid, class_table, warp, spring_z, skip_partner):
    local_count = disp.shape[0]
    block_count = lax.axis_size("gz")
    block_index = lax.axis_index("gz")
    total = local_count * block_count
    alive = valid.astype(jnp.float32)
    kappa = jnp.zeros(stiff_class.shape, jnp.float32)
    for level in range(class_table.shape[0]):
        kappa = jnp.where(stiff_class == level, class_table[level], kappa)
    kappa = kappa * alive
    depth = 1
    coeffs = extended(jnp.stack([kappa, alive]), (("tile", 2),), depth)
    global_ids = block_index * local_count + jnp.arange(local_count, dtype=jnp.int32)
    has_prev = (global_ids > 0).astype(jnp.float32)
    has_next = (global_ids < total - 1).astype(jnp.float32)
    wanted = lax.dynamic_slice_in_dim(skip_partner, block_index * local_count, local_count, 0)
    field = disp
    velocity = vel
    for step in range(ITERS):
        field_ext = extended(field, (("tile", 2),), 1)
        vel_inner = velocity
        faces = extended(field_ext, (("gz", 0),), 1)
        piece = lax.all_gather(field_ext, "gz", axis=0, tiled=True)
        count = piece.shape[0]
        inside = (wanted >= 0) & (wanted < count)
        chosen = jnp.take(piece, jnp.clip(wanted, 0, count - 1), axis=0)
        partner_ext = jnp.where(inside[:, None, None, None], chosen, jnp.zeros_like(field_ext))
        force = section_force(
            field_ext,
            coeffs[0],
            faces[:-2],
            faces[2:],
            partner_ext,
            warp,
            spring_z,
            has_prev,
            has_next,
        )
        velocity = coeffs[1][:, None, 1:-1] * (DAMPING * vel_inner + STEP * force)
        field = field_ext[:, :, 1:-1] + STEP * velocity
    return (field, velocity)


def solution(mesh):
    placed = (
        P("gz", None, "tile", None),
        P("gz", None, "tile", None),
        P("gz", "tile", None),
        P("gz", "tile", None),
        P(),
        P("gz", None, None),
        P("gz", None),
        P(),
    )
    return jax.shard_map(
        body,
        mesh=mesh,
        in_specs=placed,
        out_specs=(P("gz", None, "tile", None), P("gz", None, "tile", None)),
        check_vma=False,
    )
```

profile of v0, /device:TPU:0, one launch (start us, length us, event | category | flops | bytes accessed | tf_op | source)
XLA Modules:
  0.0 399.8 jit_solution(12897192505926920959)
XLA Ops:
  12.8 6.3 %multiply_bitcast_fusion = f32[1,2,8,5120]{3,2,1,0:T(8,128)S(1)} fusion(s32[2,8,5120]{2,1,0:T(8,128)} %param.13, s32[2,8,5120]{2,1,0:T(8,128)} %param.12, f32[]{:T(128)} %bitcast.7, f32[]{:T(128)} %bitcast.6, f32[]{:T(128)} %bitcast.5, f32[]{:T(128)} %bitcast.4, f32[]{:T(128)} %bitcast.3, f32[]{:T(128)} %bitcast.2, f32[]{:T(128)} %bitcast.1, f32[]{:T(128)} %bitcast), kind=kLoop, calls=%fused_computation.137 | loop fusion | flops 1474560 | bytes 983072 | tf_op jit(solution)/shard_map/stack | solution.py:83
  22.3 5.0 %collective-permute-start = (f32[2,2,1,5120]{3,2,1,0:T(1,128)S(1)}, f32[2,2,1,5120]{3,2,1,0:T(1,128)S(1)}, u32[]{:S(2)}, u32[]{:S(2)}) collective-permute-start(f32[2,2,1,5120]{3,2,1,0:T(1,128)S(1)} %get-tuple-element.70), channel_id=1, source_target_pairs={{0,1},{1,2},{2,3},{3,4},{4,5},{5,6},{6,7},{7,8},{8,9},{9,10},{10,1... | collective-permute-start | bytes 245768 | tf_op jit(solution)/shard_map/ppermute | solution.py:16
  34.8 6.4 %collective-permute-start.4 = (f32[1,2,10,5120]{3,1,2,0:T(2,128)S(1)}, f32[1,2,10,5120]{3,1,2,0:T(2,128)S(1)}, u32[]{:S(2)}, u32[]{:S(2)}) collective-permute-start(f32[1,2,10,5120]{3,1,2,0:T(2,128)S(1)} %copy.52), channel_id=1, source_target_pairs={{0,16},{16,32},{32,48},{48,64},{64,80},{80,96},{96,112},{1,17},{17... | collective-permute-start | bytes 1228808 | tf_op jit(solution)/shard_map/ppermute | solution.py:16
  43.3 9.2 %collective-permute-done.5 = f32[1,2,10,5120]{3,1,2,0:T(2,128)S(1)} collective-permute-done((f32[1,2,10,5120]{3,1,2,0:T(2,128)S(1)}, f32[1,2,10,5120]{3,1,2,0:T(2,128)S(1)}, u32[]{:S(2)}, u32[]{:S(2)}) %collective-permute-start.5) | collective-permute-done | bytes 409632 | tf_op jit(solution)/shard_map/ppermute | solution.py:19
  52.7 12.1 %collective-permute-done.4 = f32[1,2,10,5120]{3,1,2,0:T(2,128)S(1)} collective-permute-done((f32[1,2,10,5120]{3,1,2,0:T(2,128)S(1)}, f32[1,2,10,5120]{3,1,2,0:T(2,128)S(1)}, u32[]{:S(2)}, u32[]{:S(2)}) %collective-permute-start.4) | collective-permute-done | bytes 409632 | tf_op jit(solution)/shard_map/ppermute | solution.py:16
  66.6 2.2 fusion.97
  68.8 67.1 %all-gather.4.cloned.1.call-done = f32[16,2,10,5120]{3,1,2,0:T(2,128)} async-done(((f32[2,2,10,5120]{3,1,2,0:T(2,128)}), f32[16,2,10,5120]{3,1,2,0:T(2,128)}) %all-gather.4.cloned.1.call-update) | async-done | bytes 6553616 | tf_op jit(solution)/shard_map/all_gather | solution.py:94
  136.0 5.1 %gather_fusion = f32[2,2,10,5120]{3,1,2,0:T(2,128)} fusion(f32[16,2,10,5120]{3,1,2,0:T(2,128)} %all-gather.4.cloned.1.call-done, s32[1024]{0:T(1024)S(1)} %pad_clamp_fusion), kind=kCustom, calls=%fused_computation.clone | custom fusion | bytes 1638408 | tf_op jit(solution)/shard_map/jit(_take)/gather | solution.py:97
  143.6 3.9 multiply_add_fusion.2
  150.2 3.6 collective-permute-done.7
  157.6 6.3 %collective-permute-start.8 = (f32[1,2,10,5120]{3,1,2,0:T(2,128)S(1)}, f32[1,2,10,5120]{3,1,2,0:T(2,128)S(1)}, u32[]{:S(2)}, u32[]{:S(2)}) collective-permute-start(f32[1,2,10,5120]{3,1,2,0:T(2,128)S(1)} %copy.58), channel_id=1, source_target_pairs={{0,16},{16,32},{32,48},{48,64},{64,80},{80,96},{96,112},{1,17},{17... | collective-permute-start | bytes 1228808 | tf_op jit(solution)/shard_map/ppermute | solution.py:16
  165.2 4.8 %collective-permute-done.9 = f32[1,2,10,5120]{3,1,2,0:T(2,128)S(1)} collective-permute-done((f32[1,2,10,5120]{3,1,2,0:T(2,128)S(1)}, f32[1,2,10,5120]{3,1,2,0:T(2,128)S(1)}, u32[]{:S(2)}, u32[]{:S(2)}) %collective-permute-start.9) | collective-permute-done | bytes 409632 | tf_op jit(solution)/shard_map/ppermute | solution.py:19
  170.1 16.5 %collective-permute-done.8 = f32[1,2,10,5120]{3,1,2,0:T(2,128)S(1)} collective-permute-done((f32[1,2,10,5120]{3,1,2,0:T(2,128)S(1)}, f32[1,2,10,5120]{3,1,2,0:T(2,128)S(1)}, u32[]{:S(2)}, u32[]{:S(2)}) %collective-permute-start.8) | collective-permute-done | bytes 409632 | tf_op jit(solution)/shard_map/ppermute | solution.py:16
  190.3 69.0 %all-gather.6.cloned.1.call-done = f32[16,2,10,5120]{3,1,2,0:T(2,128)} async-done(((f32[2,2,10,5120]{3,1,2,0:T(2,128)}), f32[16,2,10,5120]{3,1,2,0:T(2,128)}) %all-gather.6.cloned.1.call-update) | async-done | bytes 6553616 | tf_op jit(solution)/shard_map/all_gather | solution.py:94
  259.2 5.1 %gather_fusion.1 = f32[2,2,10,5120]{3,1,2,0:T(2,128)} fusion(f32[16,2,10,5120]{3,1,2,0:T(2,128)} %all-gather.6.cloned.1.call-done, s32[1024]{0:T(1024)S(1)} %pad_clamp_fusion), kind=kCustom, calls=%fused_computation.1.clone | custom fusion | bytes 1638408 | tf_op jit(solution)/shard_map/jit(_take)/gather | solution.py:97
  266.9 3.9 multiply_add_fusion.1
  273.5 3.6 collective-permute-done.11
  280.8 6.1 %collective-permute-start.12 = (f32[1,2,10,5120]{3,1,2,0:T(2,128)S(1)}, f32[1,2,10,5120]{3,1,2,0:T(2,128)S(1)}, u32[]{:S(2)}, u32[]{:S(2)}) collective-permute-start(f32[1,2,10,5120]{3,1,2,0:T(2,128)S(1)} %copy.64), channel_id=1, source_target_pairs={{0,16},{16,32},{32,48},{48,64},{64,80},{80,96},{96,112},{1,17},{17... | collective-permute-start | bytes 1228808 | tf_op jit(solution)/shard_map/ppermute | solution.py:16
  288.2 5.0 %collective-permute-done.13 = f32[1,2,10,5120]{3,1,2,0:T(2,128)S(1)} collective-permute-done((f32[1,2,10,5120]{3,1,2,0:T(2,128)S(1)}, f32[1,2,10,5120]{3,1,2,0:T(2,128)S(1)}, u32[]{:S(2)}, u32[]{:S(2)}) %collective-permute-start.13) | collective-permute-done | bytes 409632 | tf_op jit(solution)/shard_map/ppermute | solution.py:19
  293.3 16.5 %collective-permute-done.12 = f32[1,2,10,5120]{3,1,2,0:T(2,128)S(1)} collective-permute-done((f32[1,2,10,5120]{3,1,2,0:T(2,128)S(1)}, f32[1,2,10,5120]{3,1,2,0:T(2,128)S(1)}, u32[]{:S(2)}, u32[]{:S(2)}) %collective-permute-start.12) | collective-permute-done | bytes 409632 | tf_op jit(solution)/shard_map/ppermute | solution.py:16
  310.3 1.8 fusion.93
  313.6 68.8 %all-gather.8.cloned.1.call-done = f32[16,2,10,5120]{3,1,2,0:T(2,128)} async-done(((f32[2,2,10,5120]{3,1,2,0:T(2,128)}), f32[16,2,10,5120]{3,1,2,0:T(2,128)}) %all-gather.8.cloned.1.call-update) | async-done | bytes 6553616 | tf_op jit(solution)/shard_map/all_gather | solution.py:94
  382.5 4.4 %gather_fusion.2 = f32[2,2,10,5120]{3,1,2,0:T(2,128)S(1)} fusion(f32[16,2,10,5120]{3,1,2,0:T(2,128)} %all-gather.8.cloned.1.call-done, s32[1024]{0:T(1024)} %copy-done.49), kind=kCustom, calls=%fused_computation.2.clone | custom fusion | bytes 1638408 | tf_op jit(solution)/shard_map/jit(_take)/gather | solution.py:97
  389.2 4.1 %multiply_add_fusion = (f32[2,2,8,5120]{3,2,1,0:T(8,128)}, f32[2,2,8,5120]{3,2,1,0:T(8,128)}) fusion(f32[2,2,8,5120]{3,2,1,0:T(8,128)S(1)} %get-tuple-element.18, f32[2,2,8,5119]{3,2,1,0:T(8,128)S(1)} %get-tuple-element.39, f32[2]{0:T(128)S(1)} %get-tuple-element.86, f32[2,2,10,5120]{3,2,1,0:T(8,128)S(1)} %fusion, f32[2]{0:T(128)S(1)} %get-tuple-element.85, ...), kind=kLoop, calls=%fused_computation.132 | loop fusion | flops 8192000 | bytes 13925496 | tf_op jit(solution)/shard_map/add | solution.py:111
  (179 shorter events, 48.5 us)
Async XLA Ops:
  7.2 128.8 %all-gather.4.cloned.1.call-start = ((), (), s32[]{:S(2)}) async-start(), calls=%async_computation | async-start | bytes 7372800 | tf_op jit(solution)/shard_map/all_gather | solution.py:94
  8.6 10.5 %collective-permute-start.2 = (f32[2,2,1,5120]{3,2,1,0:T(1,128)S(1)}, f32[2,2,1,5120]{3,2,1,0:T(1,128)S(1)}, u32[]{:S(2)}, u32[]{:S(2)}) collective-permute-start(f32[2,2,1,5120]{3,2,1,0:T(1,128)S(1)} %get-tuple-element.72), channel_id=1, source_target_pairs={{0,1},{1,2},{2,3},{3,4},{4,5},{5,6},{6,7},{7,8},{8,9},{9,10},{10,1... | collective-permute-start | bytes 245768 | tf_op jit(solution)/shard_map/ppermute | solution.py:16
  9.9 9.2 %collective-permute-start.3 = (f32[2,2,1,5120]{3,2,1,0:T(1,128)S(1)}, f32[2,2,1,5120]{3,2,1,0:T(1,128)S(1)}, u32[]{:S(2)}, u32[]{:S(2)}) collective-permute-start(f32[2,2,1,5120]{3,2,1,0:T(1,128)S(1)} %get-tuple-element.73), channel_id=1, source_target_pairs={{1,0},{2,1},{3,2},{4,3},{5,4},{6,5},{7,6},{8,7},{9,8},{10,9},{11,1... | collective-permute-start | bytes 245768 | tf_op jit(solution)/shard_map/ppermute | solution.py:19
  22.1 237.2 %all-gather.6.cloned.1.call-start = ((), (), s32[]{:S(2)}) async-start(), calls=%async_computation.1 | async-start | bytes 7372800 | tf_op jit(solution)/shard_map/all_gather | solution.py:94
  22.3 8.1 %collective-permute-start = (f32[2,2,1,5120]{3,2,1,0:T(1,128)S(1)}, f32[2,2,1,5120]{3,2,1,0:T(1,128)S(1)}, u32[]{:S(2)}, u32[]{:S(2)}) collective-permute-start(f32[2,2,1,5120]{3,2,1,0:T(1,128)S(1)} %get-tuple-element.70), channel_id=1, source_target_pairs={{0,1},{1,2},{2,3},{3,4},{4,5},{5,6},{6,7},{7,8},{8,9},{9,10},{10,1... | collective-permute-start | bytes 245768 | tf_op jit(solution)/shard_map/ppermute | solution.py:16
  27.2 4.4 %collective-permute-start.1 = (f32[2,2,1,5120]{3,2,1,0:T(1,128)S(1)}, f32[2,2,1,5120]{3,2,1,0:T(1,128)S(1)}, u32[]{:S(2)}, u32[]{:S(2)}) collective-permute-start(f32[2,2,1,5120]{3,2,1,0:T(1,128)S(1)} %get-tuple-element.71), channel_id=1, source_target_pairs={{1,0},{2,1},{3,2},{4,3},{5,4},{6,5},{7,6},{8,7},{9,8},{10,9},{11,1... | collective-permute-start | bytes 245768 | tf_op jit(solution)/shard_map/ppermute | solution.py:19
  29.0 237.5 %copy-start.39 = (f32[2]{0:T(128)}, f32[2]{0:T(128)S(1)}, u32[]{:S(2)}) copy-start(f32[2]{0:T(128)S(1)} %get-tuple-element.76) | copy-start | bytes 28
  29.1 237.5 %copy-start.41 = (f32[2]{0:T(128)}, f32[2]{0:T(128)S(1)}, u32[]{:S(2)}) copy-start(f32[2]{0:T(128)S(1)} %get-tuple-element.77) | copy-start | bytes 28
  29.1 237.5 %copy-start.43 = (f32[2]{0:T(128)}, f32[2]{0:T(128)S(1)}, u32[]{:S(2)}) copy-start(f32[2]{0:T(128)S(1)} %get-tuple-element.78) | copy-start | bytes 28
  29.1 237.5 %copy-start.45 = (f32[2]{0:T(128)}, f32[2]{0:T(128)S(1)}, u32[]{:S(2)}) copy-start(f32[2]{0:T(128)S(1)} %get-tuple-element.79) | copy-start | bytes 28
  29.1 237.4 %copy-start.33 = (f32[2]{0:T(128)}, f32[2]{0:T(128)S(1)}, u32[]{:S(2)}) copy-start(f32[2]{0:T(128)S(1)} %get-tuple-element.98) | copy-start | bytes 28
  29.1 237.4 %copy-start.35 = (f32[2]{0:T(128)}, f32[2]{0:T(128)S(1)}, u32[]{:S(2)}) copy-start(f32[2]{0:T(128)S(1)} %get-tuple-element.99) | copy-start | bytes 28
  29.1 237.4 %copy-start.37 = (f32[2]{0:T(128)}, f32[2]{0:T(128)S(1)}, u32[]{:S(2)}) copy-start(f32[2]{0:T(128)S(1)} %get-tuple-element.100) | copy-start | bytes 28
  33.5 19.1 %collective-permute-start.5 = (f32[1,2,10,5120]{3,1,2,0:T(2,128)S(1)}, f32[1,2,10,5120]{3,1,2,0:T(2,128)S(1)}, u32[]{:S(2)}, u32[]{:S(2)}) collective-permute-start(f32[1,2,10,5120]{3,1,2,0:T(2,128)S(1)} %copy.54), channel_id=1, source_target_pairs={{16,0},{32,16},{48,32},{64,48},{80,64},{96,80},{112,96},{17,1},{33... | collective-permute-start | bytes 1228808 | tf_op jit(solution)/shard_map/ppermute | solution.py:19
  34.8 30.0 %collective-permute-start.4 = (f32[1,2,10,5120]{3,1,2,0:T(2,128)S(1)}, f32[1,2,10,5120]{3,1,2,0:T(2,128)S(1)}, u32[]{:S(2)}, u32[]{:S(2)}) collective-permute-start(f32[1,2,10,5120]{3,1,2,0:T(2,128)S(1)} %copy.52), channel_id=1, source_target_pairs={{0,16},{16,32},{32,48},{48,64},{64,80},{80,96},{96,112},{1,17},{17... | collective-permute-start | bytes 1228808 | tf_op jit(solution)/shard_map/ppermute | solution.py:16
  147.6 2.6 collective-permute-start.6
  148.9 4.9 %collective-permute-start.7 = (f32[2,2,1,5120]{3,2,1,0:T(1,128)S(1)}, f32[2,2,1,5120]{3,2,1,0:T(1,128)S(1)}, u32[]{:S(2)}, u32[]{:S(2)}) collective-permute-start(f32[2,2,1,5120]{3,2,1,0:T(1,128)S(1)} %get-tuple-element.63), channel_id=1, source_target_pairs={{1,0},{2,1},{3,2},{4,3},{5,4},{6,5},{7,6},{8,7},{9,8},{10,9},{11,1... | collective-permute-start | bytes 245768 | tf_op jit(solution)/shard_map/ppermute | solution.py:19
  155.5 226.9 %all-gather.8.cloned.1.call-start = ((), (), s32[]{:S(2)}) async-start(), calls=%async_computation.2 | async-start | bytes 7372800 | tf_op jit(solution)/shard_map/all_gather | solution.py:94
  156.3 13.6 %collective-permute-start.9 = (f32[1,2,10,5120]{3,1,2,0:T(2,128)S(1)}, f32[1,2,10,5120]{3,1,2,0:T(2,128)S(1)}, u32[]{:S(2)}, u32[]{:S(2)}) collective-permute-start(f32[1,2,10,5120]{3,1,2,0:T(2,128)S(1)} %copy.60), channel_id=1, source_target_pairs={{16,0},{32,16},{48,32},{64,48},{80,64},{96,80},{112,96},{17,1},{33... | collective-permute-start | bytes 1228808 | tf_op jit(solution)/shard_map/ppermute | solution.py:19
  157.6 29.0 %collective-permute-start.8 = (f32[1,2,10,5120]{3,1,2,0:T(2,128)S(1)}, f32[1,2,10,5120]{3,1,2,0:T(2,128)S(1)}, u32[]{:S(2)}, u32[]{:S(2)}) collective-permute-start(f32[1,2,10,5120]{3,1,2,0:T(2,128)S(1)} %copy.58), channel_id=1, source_target_pairs={{0,16},{16,32},{32,48},{48,64},{64,80},{80,96},{96,112},{1,17},{17... | collective-permute-start | bytes 1228808 | tf_op jit(solution)/shard_map/ppermute | solution.py:16
  270.8 2.6 collective-permute-start.10
  272.1 4.9 %collective-permute-start.11 = (f32[2,2,1,5120]{3,2,1,0:T(1,128)S(1)}, f32[2,2,1,5120]{3,2,1,0:T(1,128)S(1)}, u32[]{:S(2)}, u32[]{:S(2)}) collective-permute-start(f32[2,2,1,5120]{3,2,1,0:T(1,128)S(1)} %get-tuple-element.59), channel_id=1, source_target_pairs={{1,0},{2,1},{3,2},{4,3},{5,4},{6,5},{7,6},{8,7},{9,8},{10,9},{11,1... | collective-permute-start | bytes 245768 | tf_op jit(solution)/shard_map/ppermute | solution.py:19
  279.5 13.6 %collective-permute-start.13 = (f32[1,2,10,5120]{3,1,2,0:T(2,128)S(1)}, f32[1,2,10,5120]{3,1,2,0:T(2,128)S(1)}, u32[]{:S(2)}, u32[]{:S(2)}) collective-permute-start(f32[1,2,10,5120]{3,1,2,0:T(2,128)S(1)} %copy.66), channel_id=1, source_target_pairs={{16,0},{32,16},{48,32},{64,48},{80,64},{96,80},{112,96},{17,1},{33... | collective-permute-start | bytes 1228808 | tf_op jit(solution)/shard_map/ppermute | solution.py:19
  280.8 29.0 %collective-permute-start.12 = (f32[1,2,10,5120]{3,1,2,0:T(2,128)S(1)}, f32[1,2,10,5120]{3,1,2,0:T(2,128)S(1)}, u32[]{:S(2)}, u32[]{:S(2)}) collective-permute-start(f32[1,2,10,5120]{3,1,2,0:T(2,128)S(1)} %copy.64), channel_id=1, source_target_pairs={{0,16},{16,32},{32,48},{48,64},{64,80},{80,96},{96,112},{1,17},{17... | collective-permute-start | bytes 1228808 | tf_op jit(solution)/shard_map/ppermute | solution.py:16
  (44 other events, 840.8 us)
Sparse Core Ops, SparseCore 0:
  22.2 113.7 all-gather.3
  155.7 103.5 all-gather.5
  278.9 103.4 all-gather.7
where the time goes:
time: 401 us; the launch traced here: 400 us
  waiting for transfers between devices  277 us (69%)
  local copies, waits for them, and re-layouts  45.2 us (11%)
  starting transfers between devices  36.8 us (9%)
  other arithmetic  25.7 us (6%)
  between operations  14.7 us (4%)
    all_gather x3, waiting for transfers between devices, body(): piece = lax.all_gather(field_ext, 'gz', axis=0, tiled=True)  205 us
    ppermute x7, waiting for transfers between devices, extended(): lax.ppermute(lax.slice_in_dim(block, block.shape[dim] - width, None, axis...  45.1 us
    ppermute x7, starting transfers between devices, extended(): lax.ppermute(lax.slice_in_dim(block, block.shape[dim] - width, None, axis...  27.6 us
    ppermute x7, waiting for transfers between devices, extended(): lax.ppermute(lax.slice_in_dim(block, 0, width, axis=dim), axis, backward)  27.3 us
    gather x3, local copies, waits for them, and re-layouts, body(): chosen = jnp.take(piece, jnp.clip(wanted, 0, count - 1), axis=0)  14.6 us
    add x3, other arithmetic, body(): field = field_ext[:, :, 1:-1] + STEP * velocity  11.8 us
    slice x8, local copies, waits for them, and re-layouts, shift_left(): field[..., 1:]  9.89 us
    ppermute x7, starting transfers between devices, extended(): lax.ppermute(lax.slice_in_dim(block, 0, width, axis=dim), axis, backward)  9.04 us
  transfers between devices with their start and end apart: 17, of which 12 were waited for; matrix products, arithmetic and copies ran while one was open for 7% of the time, Pallas kernels for 0%

commit v1 on v0

--- a/solution.py
+++ b/solution.py
@@ -91,7 +91,10 @@
         field_ext = extended(field, (("tile", 2),), 1)
         vel_inner = velocity
         faces = extended(field_ext, (("gz", 0),), 1)
-        piece = lax.all_gather(field_ext, "gz", axis=0, tiled=True)
+        reached = lax.axis_size("gz")
+        extra = jnp.stack(reached * [field_ext])
+        aux = lax.all_to_all(extra, axis_name="gz", split_axis=0, concat_axis=0)
+        piece = jnp.concatenate(aux, axis=0)
         count = piece.shape[0]
         inside = (wanted >= 0) & (wanted < count)
         chosen = jnp.take(piece, jnp.clip(wanted, 0, count - 1), axis=0)

time: 401 us -> 429 us (1.070)
  the two profiles are of different devices: /device:TPU:0 before, /device:TPU:31 now
where the time goes in v1:
time: 429 us; the launch traced here: 428 us
  waiting for transfers between devices  267 us (62%)
  starting transfers between devices  71.1 us (17%)
  local copies, waits for them, and re-layouts  60.7 us (14%)
  other arithmetic  28.2 us (7%)
    ppermute x7, waiting for transfers between devices, extended(): lax.ppermute(lax.slice_in_dim(block, block.shape[dim] - width, None, axis...  266 us
    ppermute x7, starting transfers between devices, extended(): lax.ppermute(lax.slice_in_dim(block, block.shape[dim] - width, None, axis...  34.8 us
    ppermute x7, starting transfers between devices, extended(): lax.ppermute(lax.slice_in_dim(block, 0, width, axis=dim), axis, backward)  19.4 us
    all_to_all x3, starting transfers between devices, body(): aux = lax.all_to_all(extra, axis_name='gz', split_axis=0, concat_axis=0)  17 us
    another operation x3, local copies, waits for them, and re-layouts, body(): extra = jnp.stack(reached * [field_ext])  15.9 us
    gather x3, local copies, waits for them, and re-layouts, body(): chosen = jnp.take(piece, jnp.clip(wanted, 0, count - 1), axis=0)  15 us
    add x3, other arithmetic, body(): field = field_ext[:, :, 1:-1] + STEP * velocity  11.9 us
    slice x8, local copies, waits for them, and re-layouts, shift_left(): field[..., 1:]  9.28 us
  transfers between devices with their start and end apart: 17, of which 6 were waited for; matrix products, arithmetic and copies ran while one was open for 9% of the time, Pallas kernels for 0%

profile of v1, /device:TPU:31, one launch (start us, length us, event | category | flops | bytes accessed | tf_op | source)
XLA Modules:
  0.0 428.1 jit_solution(10808166296030221357)
XLA Ops:
  4.7 5.1 %collective-permute-start.2 = (f32[2,2,1,5120]{3,2,1,0:T(1,128)S(1)}, f32[2,2,1,5120]{3,2,1,0:T(1,128)S(1)}, u32[]{:S(2)}, u32[]{:S(2)}) collective-permute-start(f32[2,2,1,5120]{3,2,1,0:T(1,128)S(1)} %get-tuple-element.70), channel_id=1, source_target_pairs={{0,1},{1,2},{2,3},{3,4},{4,5},{5,6},{6,7},{7,8},{8,9},{9,10},{10,1... | collective-permute-start | bytes 245768 | tf_op jit(solution)/shard_map/ppermute | solution.py:16
  12.4 6.4 %multiply_bitcast_fusion = f32[1,2,8,5120]{3,2,1,0:T(8,128)S(1)} fusion(s32[2,8,5120]{2,1,0:T(8,128)} %param.13, s32[2,8,5120]{2,1,0:T(8,128)} %param.12, f32[]{:T(128)} %bitcast.7, f32[]{:T(128)} %bitcast.6, f32[]{:T(128)} %bitcast.5, f32[]{:T(128)} %bitcast.4, f32[]{:T(128)} %bitcast.3, f32[]{:T(128)} %bitcast.2, f32[]{:T(128)} %bitcast.1, f32[]{:T(128)} %bitcast), kind=kLoop, calls=%fused_computation.137 | loop fusion | flops 1474560 | bytes 983072 | tf_op jit(solution)/shard_map/stack | solution.py:83
  20.9 5.8 %collective-permute-start = (f32[2,2,1,5120]{3,2,1,0:T(1,128)S(1)}, f32[2,2,1,5120]{3,2,1,0:T(1,128)S(1)}, u32[]{:S(2)}, u32[]{:S(2)}) collective-permute-start(f32[2,2,1,5120]{3,2,1,0:T(1,128)S(1)} %get-tuple-element.68), channel_id=1, source_target_pairs={{0,1},{1,2},{2,3},{3,4},{4,5},{5,6},{6,7},{7,8},{8,9},{9,10},{10,1... | collective-permute-start | bytes 245768 | tf_op jit(solution)/shard_map/ppermute | solution.py:16
  31.7 5.3 %stack.15 = f32[8,2,2,10,5120]{4,2,3,1,0:T(2,128)} broadcast(f32[2,2,10,5120]{3,1,2,0:T(2,128)S(1)} %copy.38), dimensions={1,2,3,4} | broadcast | bytes 7372800 | tf_op jit(solution)/shard_map/stack | solution.py:95
  37.0 7.5 %all-to-all-start = ((f32[8,2,2,10,5120]{4,2,3,1,0:T(2,128)}), f32[8,2,2,10,5120]{4,2,3,1,0:T(2,128)}, u32[]{:S(2)}, u32[]{:S(2)}) async-start(f32[8,2,2,10,5120]{4,2,3,1,0:T(2,128)} %stack.15), calls=%async_computation | async-start | bytes 13107200 | tf_op jit(solution)/shard_map/all_to_all | solution.py:96
  44.9 4.6 %collective-permute-start.4 = (f32[1,2,10,5120]{3,1,2,0:T(2,128)S(1)}, f32[1,2,10,5120]{3,1,2,0:T(2,128)S(1)}, u32[]{:S(2)}, u32[]{:S(2)}) collective-permute-start(f32[1,2,10,5120]{3,1,2,0:T(2,128)S(1)} %copy.34), channel_id=1, source_target_pairs={{0,16},{16,32},{32,48},{48,64},{64,80},{80,96},{96,112},{1,17},{17... | collective-permute-start | bytes 1228808 | tf_op jit(solution)/shard_map/ppermute | solution.py:16
  56.2 84.7 %collective-permute-done.4 = f32[1,2,10,5120]{3,1,2,0:T(2,128)S(1)} collective-permute-done((f32[1,2,10,5120]{3,1,2,0:T(2,128)S(1)}, f32[1,2,10,5120]{3,1,2,0:T(2,128)S(1)}, u32[]{:S(2)}, u32[]{:S(2)}) %collective-permute-start.4) | collective-permute-done | bytes 409632 | tf_op jit(solution)/shard_map/ppermute | solution.py:16
  145.0 5.3 %gather_fusion = f32[2,2,10,5120]{3,1,2,0:T(2,128)} fusion(f32[16,2,10,5120]{3,1,2,0:T(2,128)} %bitcast.15, s32[1024]{0:T(1024)} %pad_clamp_fusion), kind=kCustom, calls=%fused_computation.clone | custom fusion | bytes 1638408 | tf_op jit(solution)/shard_map/jit(_take)/gather | solution.py:100
  152.9 4.0 multiply_add_fusion.2
  158.9 5.9 %collective-permute-start.6 = (f32[2,2,1,5120]{3,2,1,0:T(1,128)S(1)}, f32[2,2,1,5120]{3,2,1,0:T(1,128)S(1)}, u32[]{:S(2)}, u32[]{:S(2)}) collective-permute-start(f32[2,2,1,5120]{3,2,1,0:T(1,128)S(1)} %get-tuple-element.60), channel_id=1, source_target_pairs={{0,1},{1,2},{2,3},{3,4},{4,5},{5,6},{6,7},{7,8},{8,9},{9,10},{10,1... | collective-permute-start | bytes 245768 | tf_op jit(solution)/shard_map/ppermute | solution.py:16
  167.0 5.3 %stack.16 = f32[8,2,2,10,5120]{4,2,3,1,0:T(2,128)} broadcast(f32[2,2,10,5120]{3,1,2,0:T(2,128)S(1)} %copy.44), dimensions={1,2,3,4} | broadcast | bytes 7372800 | tf_op jit(solution)/shard_map/stack | solution.py:95
  172.3 4.7 %all-to-all-start.1 = ((f32[8,2,2,10,5120]{4,2,3,1,0:T(2,128)}), f32[8,2,2,10,5120]{4,2,3,1,0:T(2,128)}, u32[]{:S(2)}, u32[]{:S(2)}) async-start(f32[8,2,2,10,5120]{4,2,3,1,0:T(2,128)} %stack.16), calls=%async_computation.1 | async-start | bytes 13107200 | tf_op jit(solution)/shard_map/all_to_all | solution.py:96
  177.4 4.0 collective-permute-start.8
  186.7 89.8 %collective-permute-done.8 = f32[1,2,10,5120]{3,1,2,0:T(2,128)S(1)} collective-permute-done((f32[1,2,10,5120]{3,1,2,0:T(2,128)S(1)}, f32[1,2,10,5120]{3,1,2,0:T(2,128)S(1)}, u32[]{:S(2)}, u32[]{:S(2)}) %collective-permute-start.8) | collective-permute-done | bytes 409632 | tf_op jit(solution)/shard_map/ppermute | solution.py:16
  281.4 5.3 %gather_fusion.1 = f32[2,2,10,5120]{3,1,2,0:T(2,128)} fusion(f32[16,2,10,5120]{3,1,2,0:T(2,128)} %bitcast.16, s32[1024]{0:T(1024)} %pad_clamp_fusion), kind=kCustom, calls=%fused_computation.1.clone | custom fusion | bytes 1638408 | tf_op jit(solution)/shard_map/jit(_take)/gather | solution.py:100
  289.2 3.9 multiply_add_fusion.1
  295.5 5.4 %collective-permute-start.10 = (f32[2,2,1,5120]{3,2,1,0:T(1,128)S(1)}, f32[2,2,1,5120]{3,2,1,0:T(1,128)S(1)}, u32[]{:S(2)}, u32[]{:S(2)}) collective-permute-start(f32[2,2,1,5120]{3,2,1,0:T(1,128)S(1)} %get-tuple-element.56), channel_id=1, source_target_pairs={{0,1},{1,2},{2,3},{3,4},{4,5},{5,6},{6,7},{7,8},{8,9},{9,10},{10,1... | collective-permute-start | bytes 245768 | tf_op jit(solution)/shard_map/ppermute | solution.py:16
  303.2 5.3 %stack.17 = f32[8,2,2,10,5120]{4,2,3,1,0:T(2,128)} broadcast(f32[2,2,10,5120]{3,1,2,0:T(2,128)S(1)} %copy.50), dimensions={1,2,3,4} | broadcast | bytes 7372800 | tf_op jit(solution)/shard_map/stack | solution.py:95
  308.5 4.7 %all-to-all-start.2 = ((f32[8,2,2,10,5120]{4,2,3,1,0:T(2,128)}), f32[8,2,2,10,5120]{4,2,3,1,0:T(2,128)}, u32[]{:S(2)}, u32[]{:S(2)}) async-start(f32[8,2,2,10,5120]{4,2,3,1,0:T(2,128)} %stack.17), calls=%async_computation.2 | async-start | bytes 13107200 | tf_op jit(solution)/shard_map/all_to_all | solution.py:96
  313.7 4.0 collective-permute-start.12
  318.1 3.9 collective-permute-start.13
  323.2 89.2 %collective-permute-done.12 = f32[1,2,10,5120]{3,1,2,0:T(2,128)S(1)} collective-permute-done((f32[1,2,10,5120]{3,1,2,0:T(2,128)S(1)}, f32[1,2,10,5120]{3,1,2,0:T(2,128)S(1)}, u32[]{:S(2)}, u32[]{:S(2)}) %collective-permute-start.12) | collective-permute-done | bytes 409632 | tf_op jit(solution)/shard_map/ppermute | solution.py:16
  417.3 4.4 %gather_fusion.2 = f32[2,2,10,5120]{3,1,2,0:T(2,128)S(1)} fusion(f32[16,2,10,5120]{3,1,2,0:T(2,128)} %bitcast.17, s32[1024]{0:T(1024)} %pad_clamp_fusion), kind=kCustom, calls=%fused_computation.2.clone | custom fusion | bytes 1638408 | tf_op jit(solution)/shard_map/jit(_take)/gather | solution.py:100
  424.1 4.1 multiply_add_fusion
  (175 shorter events, 57.9 us)
Async XLA Ops:
  0.6 26.1 %copy-start = (f32[2,2,8,5120]{3,2,1,0:T(8,128)S(1)}, f32[2,2,8,5120]{3,2,1,0:T(8,128)}, u32[]{:S(2)}) copy-start(f32[2,2,8,5120]{3,2,1,0:T(8,128)} %param.10) | copy-start | bytes 1966084
  2.1 28.7 %collective-permute-start.3 = (f32[2,2,1,5120]{3,2,1,0:T(1,128)S(1)}, f32[2,2,1,5120]{3,2,1,0:T(1,128)S(1)}, u32[]{:S(2)}, u32[]{:S(2)}) collective-permute-start(f32[2,2,1,5120]{3,2,1,0:T(1,128)S(1)} %get-tuple-element.71), channel_id=1, source_target_pairs={{1,0},{2,1},{3,2},{4,3},{5,4},{6,5},{7,6},{8,7},{9,8},{10,9},{11,1... | collective-permute-start | bytes 245768 | tf_op jit(solution)/shard_map/ppermute | solution.py:19
  4.7 26.1 %collective-permute-start.2 = (f32[2,2,1,5120]{3,2,1,0:T(1,128)S(1)}, f32[2,2,1,5120]{3,2,1,0:T(1,128)S(1)}, u32[]{:S(2)}, u32[]{:S(2)}) collective-permute-start(f32[2,2,1,5120]{3,2,1,0:T(1,128)S(1)} %get-tuple-element.70), channel_id=1, source_target_pairs={{0,1},{1,2},{2,3},{3,4},{4,5},{5,6},{6,7},{7,8},{8,9},{9,10},{10,1... | collective-permute-start | bytes 245768 | tf_op jit(solution)/shard_map/ppermute | solution.py:16
  18.9 9.1 %copy-start.30 = (f32[2,3,2]{1,2,0:T(2,128)S(1)}, f32[2,3,2]{1,2,0:T(2,128)}, u32[]{:S(2)}) copy-start(f32[2,3,2]{1,2,0:T(2,128)} %param.15) | copy-start | bytes 148
  18.9 9.3 %copy-start.31 = (f32[2,3]{1,0:T(2,128)S(1)}, f32[2,3]{1,0:T(2,128)}, u32[]{:S(2)}) copy-start(f32[2,3]{1,0:T(2,128)} %param.16) | copy-start | bytes 76
  18.9 9.5 %copy-start.48 = (s32[16]{0:T(128)S(1)}, s32[16]{0:T(128)}, u32[]{:S(2)}) copy-start(s32[16]{0:T(128)} %param.17) | copy-start | bytes 196
  19.0 33.9 %collective-permute-start.1 = (f32[2,2,1,5120]{3,2,1,0:T(1,128)S(1)}, f32[2,2,1,5120]{3,2,1,0:T(1,128)S(1)}, u32[]{:S(2)}, u32[]{:S(2)}) collective-permute-start(f32[2,2,1,5120]{3,2,1,0:T(1,128)S(1)} %get-tuple-element.69), channel_id=1, source_target_pairs={{1,0},{2,1},{3,2},{4,3},{5,4},{6,5},{7,6},{8,7},{9,8},{10,9},{11,1... | collective-permute-start | bytes 245768 | tf_op jit(solution)/shard_map/ppermute | solution.py:19
  20.9 32.0 %collective-permute-start = (f32[2,2,1,5120]{3,2,1,0:T(1,128)S(1)}, f32[2,2,1,5120]{3,2,1,0:T(1,128)S(1)}, u32[]{:S(2)}, u32[]{:S(2)}) collective-permute-start(f32[2,2,1,5120]{3,2,1,0:T(1,128)S(1)} %get-tuple-element.68), channel_id=1, source_target_pairs={{0,1},{1,2},{2,3},{3,4},{4,5},{5,6},{6,7},{7,8},{8,9},{9,10},{10,1... | collective-permute-start | bytes 245768 | tf_op jit(solution)/shard_map/ppermute | solution.py:16
  37.0 108.0 %all-to-all-start = ((f32[8,2,2,10,5120]{4,2,3,1,0:T(2,128)}), f32[8,2,2,10,5120]{4,2,3,1,0:T(2,128)}, u32[]{:S(2)}, u32[]{:S(2)}) async-start(f32[8,2,2,10,5120]{4,2,3,1,0:T(2,128)} %stack.15), calls=%async_computation | async-start | bytes 13107200 | tf_op jit(solution)/shard_map/all_to_all | solution.py:96
  44.9 95.9 %collective-permute-start.4 = (f32[1,2,10,5120]{3,1,2,0:T(2,128)S(1)}, f32[1,2,10,5120]{3,1,2,0:T(2,128)S(1)}, u32[]{:S(2)}, u32[]{:S(2)}) collective-permute-start(f32[1,2,10,5120]{3,1,2,0:T(2,128)S(1)} %copy.34), channel_id=1, source_target_pairs={{0,16},{16,32},{32,48},{48,64},{64,80},{80,96},{96,112},{1,17},{17... | collective-permute-start | bytes 1228808 | tf_op jit(solution)/shard_map/ppermute | solution.py:16
  49.8 91.2 %collective-permute-start.5 = (f32[1,2,10,5120]{3,1,2,0:T(2,128)S(1)}, f32[1,2,10,5120]{3,1,2,0:T(2,128)S(1)}, u32[]{:S(2)}, u32[]{:S(2)}) collective-permute-start(f32[1,2,10,5120]{3,1,2,0:T(2,128)S(1)} %copy.36), channel_id=1, source_target_pairs={{16,0},{32,16},{48,32},{64,48},{80,64},{96,80},{112,96},{17,1},{33... | collective-permute-start | bytes 1228808 | tf_op jit(solution)/shard_map/ppermute | solution.py:19
  145.0 5.3 %copy-start.46 = (pred[2]{0:T(512)(128)(4,1)S(1)}, pred[2]{0:T(512)(128)(4,1)}, u32[]{:S(2)}) copy-start(pred[2]{0:T(512)(128)(4,1)} %get-tuple-element.20) | copy-start | bytes 10
  145.0 5.3 %copy-start.47 = (pred[2]{0:T(512)(128)(4,1)S(1)}, pred[2]{0:T(512)(128)(4,1)}, u32[]{:S(2)}) copy-start(pred[2]{0:T(512)(128)(4,1)} %get-tuple-element.94) | copy-start | bytes 10
  156.9 7.9 %collective-permute-start.7 = (f32[2,2,1,5120]{3,2,1,0:T(1,128)S(1)}, f32[2,2,1,5120]{3,2,1,0:T(1,128)S(1)}, u32[]{:S(2)}, u32[]{:S(2)}) collective-permute-start(f32[2,2,1,5120]{3,2,1,0:T(1,128)S(1)} %get-tuple-element.61), channel_id=1, source_target_pairs={{1,0},{2,1},{3,2},{4,3},{5,4},{6,5},{7,6},{8,7},{9,8},{10,9},{11,1... | collective-permute-start | bytes 245768 | tf_op jit(solution)/shard_map/ppermute | solution.py:19
  158.9 7.2 %collective-permute-start.6 = (f32[2,2,1,5120]{3,2,1,0:T(1,128)S(1)}, f32[2,2,1,5120]{3,2,1,0:T(1,128)S(1)}, u32[]{:S(2)}, u32[]{:S(2)}) collective-permute-start(f32[2,2,1,5120]{3,2,1,0:T(1,128)S(1)} %get-tuple-element.60), channel_id=1, source_target_pairs={{0,1},{1,2},{2,3},{3,4},{4,5},{5,6},{6,7},{7,8},{8,9},{9,10},{10,1... | collective-permute-start | bytes 245768 | tf_op jit(solution)/shard_map/ppermute | solution.py:16
  172.3 109.2 %all-to-all-start.1 = ((f32[8,2,2,10,5120]{4,2,3,1,0:T(2,128)}), f32[8,2,2,10,5120]{4,2,3,1,0:T(2,128)}, u32[]{:S(2)}, u32[]{:S(2)}) async-start(f32[8,2,2,10,5120]{4,2,3,1,0:T(2,128)} %stack.16), calls=%async_computation.1 | async-start | bytes 13107200 | tf_op jit(solution)/shard_map/all_to_all | solution.py:96
  177.4 99.1 %collective-permute-start.8 = (f32[1,2,10,5120]{3,1,2,0:T(2,128)S(1)}, f32[1,2,10,5120]{3,1,2,0:T(2,128)S(1)}, u32[]{:S(2)}, u32[]{:S(2)}) collective-permute-start(f32[1,2,10,5120]{3,1,2,0:T(2,128)S(1)} %copy.40), channel_id=1, source_target_pairs={{0,16},{16,32},{32,48},{48,64},{64,80},{80,96},{96,112},{1,17},{17... | collective-permute-start | bytes 1228808 | tf_op jit(solution)/shard_map/ppermute | solution.py:16
  181.8 94.9 %collective-permute-start.9 = (f32[1,2,10,5120]{3,1,2,0:T(2,128)S(1)}, f32[1,2,10,5120]{3,1,2,0:T(2,128)S(1)}, u32[]{:S(2)}, u32[]{:S(2)}) collective-permute-start(f32[1,2,10,5120]{3,1,2,0:T(2,128)S(1)} %copy.42), channel_id=1, source_target_pairs={{16,0},{32,16},{48,32},{64,48},{80,64},{96,80},{112,96},{17,1},{33... | collective-permute-start | bytes 1228808 | tf_op jit(solution)/shard_map/ppermute | solution.py:19
  293.2 7.9 %collective-permute-start.11 = (f32[2,2,1,5120]{3,2,1,0:T(1,128)S(1)}, f32[2,2,1,5120]{3,2,1,0:T(1,128)S(1)}, u32[]{:S(2)}, u32[]{:S(2)}) collective-permute-start(f32[2,2,1,5120]{3,2,1,0:T(1,128)S(1)} %get-tuple-element.57), channel_id=1, source_target_pairs={{1,0},{2,1},{3,2},{4,3},{5,4},{6,5},{7,6},{8,7},{9,8},{10,9},{11,1... | collective-permute-start | bytes 245768 | tf_op jit(solution)/shard_map/ppermute | solution.py:19
  295.5 6.8 %collective-permute-start.10 = (f32[2,2,1,5120]{3,2,1,0:T(1,128)S(1)}, f32[2,2,1,5120]{3,2,1,0:T(1,128)S(1)}, u32[]{:S(2)}, u32[]{:S(2)}) collective-permute-start(f32[2,2,1,5120]{3,2,1,0:T(1,128)S(1)} %get-tuple-element.56), channel_id=1, source_target_pairs={{0,1},{1,2},{2,3},{3,4},{4,5},{5,6},{6,7},{7,8},{8,9},{9,10},{10,1... | collective-permute-start | bytes 245768 | tf_op jit(solution)/shard_map/ppermute | solution.py:16
  302.4 110.4 %copy-start.28 = (f32[2,2,1,5120]{3,2,1,0:T(1,128)}, f32[2,2,1,5120]{3,2,1,0:T(1,128)S(1)}, u32[]{:S(2)}) copy-start(f32[2,2,1,5120]{3,2,1,0:T(1,128)S(1)} %collective-permute-done.10) | copy-start | bytes 245764
  308.5 108.8 %all-to-all-start.2 = ((f32[8,2,2,10,5120]{4,2,3,1,0:T(2,128)}), f32[8,2,2,10,5120]{4,2,3,1,0:T(2,128)}, u32[]{:S(2)}, u32[]{:S(2)}) async-start(f32[8,2,2,10,5120]{4,2,3,1,0:T(2,128)} %stack.17), calls=%async_computation.2 | async-start | bytes 13107200 | tf_op jit(solution)/shard_map/all_to_all | solution.py:96
  313.7 98.8 %collective-permute-start.12 = (f32[1,2,10,5120]{3,1,2,0:T(2,128)S(1)}, f32[1,2,10,5120]{3,1,2,0:T(2,128)S(1)}, u32[]{:S(2)}, u32[]{:S(2)}) collective-permute-start(f32[1,2,10,5120]{3,1,2,0:T(2,128)S(1)} %copy.46), channel_id=1, source_target_pairs={{0,16},{16,32},{32,48},{48,64},{64,80},{80,96},{96,112},{1,17},{17... | collective-permute-start | bytes 1228808 | tf_op jit(solution)/shard_map/ppermute | solution.py:16
  318.1 94.5 %collective-permute-start.13 = (f32[1,2,10,5120]{3,1,2,0:T(2,128)S(1)}, f32[1,2,10,5120]{3,1,2,0:T(2,128)S(1)}, u32[]{:S(2)}, u32[]{:S(2)}) collective-permute-start(f32[1,2,10,5120]{3,1,2,0:T(2,128)S(1)} %copy.48), channel_id=1, source_target_pairs={{16,0},{32,16},{48,32},{64,48},{80,64},{96,80},{112,96},{17,1},{33... | collective-permute-start | bytes 1228808 | tf_op jit(solution)/shard_map/ppermute | solution.py:19
  (42 other events, 88.8 us)
